TPU v7x, 256 devices: a whole 4x4x8 slice. The times are simulated.
256 devices in a mesh: section: 8 (over z), expert: 32 (over x, y, core).
Axes of the slice: x: 4, y: 4, z: 8, core: 2. Of those that a mesh axis runs over, the one named last changes fastest.
Arguments:
- emitted: bfloat16 [8, 2, 2048, 2048], P('section', None, 'expert'), may hold values from -6 to 6
- levels: int32 [8, 2, 2048], P('section', None, 'expert'), may hold values from 0 to 999
- expert_ids: int32 [8, 2, 2048, 6], P('section', None, 'expert'), may hold values from 0 to 31, all different within a row; in each aligned block of 64 rows (0 to 63, 64 to 127, ..., all dimensions but the last counted through in order) at most 16 rows name the same one
- gate_values: float32 [8, 2, 2048, 6], P('section', None, 'expert'), may hold values from 0.05 to 0.5
- w_gate: bfloat16 [8, 32, 2048, 768], P('section', 'expert'), may hold values from -0.125 to 0.125
- w_up: bfloat16 [8, 32, 2048, 768], P('section', 'expert'), may hold values from -0.125 to 0.125
- w_down: bfloat16 [8, 32, 768, 2048], P('section', 'expert'), may hold values from -0.21875 to 0.21875
- w_mod: bfloat16 [8, 256, 4096], P('section'), may hold values from -0.375 to 0.375
Outputs:
- layer_out: bfloat16 [8, 2, 2048, 2048], P('section', None, 'expert')
Inputs may be any that keep to these rules, and one draw needn't show every extreme that they name: `expert_ids`: each token names 6 different experts. Among the 64 tokens of one device of expert in one microbatch at one section, no expert is named by more than 16 tokens, and in every draw some expert is named by exactly 16 of them.
All inputs are finite; a program needn't handle non-finite values.
Results may differ from a plain program's by a relative error of at most 0.006.
Values may be sent and summed in bfloat16 or wider, within the bound.
A program may use at most 64 MiB of HBM per device.

v0:
```python
import functools
import math

import jax
import jax.numpy as jnp
from jax import lax
from jax.experimental import pallas as pl
from jax.experimental.pallas import tpu as pltpu
from jax.sharding import PartitionSpec as P

epsilon = 1e-06
MESH = pl.DeviceIdType.MESH
F32, BF16 = jnp.float32, jnp.bfloat16
SIDE = 4
SLOTS = 16
BLOCK = 64
HALF = BLOCK // 2
PICKS = SIDE * 2 * SLOTS


def level_embedding(levels, entries):
    half_width = entries // 2
    frequency = jnp.exp(-math.log(10000.0) * jnp.arange(half_width, dtype=F32) / half_width)
    angles = levels.astype(F32)[:, None] * frequency[None, :]
    return jnp.concatenate([jnp.cos(angles), jnp.sin(angles)], axis=1).astype(BF16)


def layer_kernel(
    sections, top,
    emitted, embed, ids, gates, w_gate, w_up, w_down, w_mod,
    out,
    vg, vu, vd, vm, mod, meta, weigh,
    arrived, gathered, picked, passed, rows_in, rows_out, passed_back, returned,
    parts, half_in, part_in, total,
    load_sem, z_send, z_recv, m_send, m_recv, g_send, g_recv, gf_send,
    b_send, b_recv, f_recv, f_send, o_send, o_recv, p_recv, p_send, h_send, h_recv, q_send, q_recv,
):
    section = lax.axis_index("section")
    place = lax.axis_index("expert")
    x, y, core = place // 8, (place // 2) % SIDE, place % 2
    features = arrived.shape[2]

    def at(dx, dy, other):
        seat = core + other * (1 - 2 * core)
        return (section, ((x + dx + 8) % SIDE) * 8 + ((y + dy + 8) % SIDE) * 2 + seat)

    def along(batch, da, db, other):
        return at(da + batch * (db - da), db + batch * (da - db), other)

    def remote(src, dst, send, recv, device):
        return pltpu.make_async_remote_copy(
            src_ref=src, dst_ref=dst, send_sem=send, recv_sem=recv, device_id=device, device_id_type=MESH
        )

    def got(dst, recv):
        remote(dst, dst, recv, recv, (section, place)).wait_recv()

    def left(src, send):
        remote(src, src, send, send, (section, place)).wait_send()

    after = ((section + 1) % sections, place)
    ahead = ((section + sections - 1) % sections, place)

    loads = [
        pltpu.make_async_copy(w_mod.at[0], vm, load_sem.at[0]),
        pltpu.make_async_copy(w_gate.at[0, 0], vg, load_sem.at[1]),
        pltpu.make_async_copy(w_up.at[0, 0], vu, load_sem.at[2]),
        pltpu.make_async_copy(w_down.at[0, 0], vd, load_sem.at[3]),
    ]
    loads[0].start()

    barrier = pltpu.get_barrier_semaphore()
    friends = [after, ahead, at(0, 0, 1), at(2, 0, 0), at(0, 2, 0)]
    for step in (1, -1):
        for other in (0, 1):
            friends += [at(step, 0, other), at(0, step, other)]
    for friend in friends:
        pl.semaphore_signal(barrier, inc=1, device_id=friend, device_id_type=MESH)
    pl.semaphore_wait(barrier, len(friends))

    def shift(piece):
        batch, rows = piece % 2, pl.ds(pl.multiple_of((piece // 2) * HALF, HALF), HALF)
        return remote(
            emitted.at[0, batch, rows], arrived.at[batch, rows], z_send.at[piece], z_recv.at[piece], after
        )

    for piece in range(4):
        shift(piece).start()
    for load in loads[1:]:
        load.start()

    number = ids[...]
    experts = SIDE * SIDE * 2
    name = lax.broadcasted_iota(jnp.int32, (experts, 2 * BLOCK), 0)
    named = jnp.zeros((experts, 2 * BLOCK), F32)
    for k in range(top):
        named = named + jnp.where(number[k : k + 1, :] == name, 1.0, 0.0)
    row = lax.broadcasted_iota(jnp.int32, (2 * BLOCK, 2 * BLOCK), 0)
    col = lax.broadcasted_iota(jnp.int32, (2 * BLOCK, 2 * BLOCK), 1)
    earlier = jnp.where((row < col) & (row // BLOCK == col // BLOCK), 1.0, 0.0).astype(BF16)
    before = jnp.dot(named.astype(BF16), earlier, preferred_element_type=F32)
    lane = lax.broadcasted_iota(jnp.int32, (1, 2 * BLOCK), 1)
    for batch in range(2):
        meta[batch, 0] = jnp.full((16, 2 * BLOCK), -1.0, F32)
    for k in range(top):
        slot = jnp.sum(jnp.where(number[k : k + 1, :] == name, before, 0.0), axis=0, keepdims=True)
        code = number[k : k + 1, :].astype(F32) * SLOTS + slot
        gate = gates[k : k + 1, :]
        for batch in range(2):
            mine = lane // BLOCK == batch
            shown = jnp.where(mine, code, -1.0)
            worth = jnp.where(mine, gate, 0.0)
            if batch:
                shown = pltpu.roll(shown, BLOCK, 1)
                worth = pltpu.roll(worth, BLOCK, 1)
            meta[batch, 0, k : k + 1, :] = shown
            meta[batch, 0, 8 + k : 9 + k, :] = worth

    def tell(batch, step):
        return remote(
            meta.at[batch, 0], meta.at[batch, step], m_send.at[batch, step - 1], m_recv.at[batch, step - 1],
            along(batch, step, 0, 0),
        )

    for batch in range(2):
        for step in (1, 2, 3):
            tell(batch, step).start()

    loads[0].wait()
    mod[...] = jnp.dot(embed[...], vm[...], preferred_element_type=F32)

    def spread(batch, part, way):
        rows = pl.ds(pl.multiple_of(part * HALF, HALF), HALF)
        return remote(
            gathered.at[batch, 0, rows], gathered.at[batch, 1 + 2 * way, rows],
            g_send.at[batch, way, part], g_recv.at[batch, 2 * way, part],
            along(batch, 1 - 2 * way, 0, 0),
        )

    def normalize(piece, carry):
        batch, part = piece % 2, piece // 2
        rows = pl.ds(pl.multiple_of(part * HALF, HALF), HALF)
        got(arrived.at[batch, rows], z_recv.at[piece])
        values = arrived[batch, rows, :].astype(F32)
        mean_square = jnp.mean(values * values, axis=1, keepdims=True)
        own = pl.ds(pl.multiple_of(batch * BLOCK + part * HALF, HALF), HALF)
        normed = values * lax.rsqrt(mean_square + epsilon) * (1.0 + mod[own, :features]) + mod[own, features:]
        gathered[batch, 0, rows, :] = normed.astype(BF16)
        spread(batch, part, 0).start()
        spread(batch, part, 1).start()
        return carry

    lax.fori_loop(0, 4, normalize, 0)

    def hand_on(batch, way):
        rows = pl.ds(way * HALF, HALF)
        return remote(
            gathered.at[batch, 1 + 2 * way, rows], gathered.at[batch, 2, rows],
            gf_send.at[batch, way], g_recv.at[batch, 1, way],
            along(batch, 1 - 2 * way, 0, 0),
        )

    pick = lax.broadcasted_iota(jnp.int32, (PICKS, 2 * BLOCK), 0)
    far, other, slot = pick // (2 * SLOTS), (pick // SLOTS) % 2, pick % SLOTS
    seat = core + other * (1 - 2 * core)

    def select(batch, step):
        line = jnp.where(
            batch == 0,
            x * 8 + ((y + far) % SIDE) * 2,
            ((x + far) % SIDE) * 8 + y * 2,
        )
        wanted = ((line + seat) * SLOTS + slot).astype(F32)
        hit = jnp.zeros((PICKS, 2 * BLOCK), F32)
        worth = jnp.zeros((PICKS, 2 * BLOCK), F32)
        for k in range(top):
            same = meta[batch, step, k : k + 1, :] == wanted
            hit = jnp.where(same, 1.0, hit)
            worth = jnp.where(same, meta[batch, step, 8 + k : 9 + k, :], worth)
        worth = worth.T
        high = worth[:BLOCK].astype(BF16)
        weigh[batch, step, :BLOCK, :] = high
        weigh[batch, step, BLOCK:, :] = (worth[:BLOCK] - high.astype(F32)).astype(BF16)
        chosen = jnp.dot(hit[:, :BLOCK].astype(BF16), gathered[batch, step], preferred_element_type=F32)
        picked[batch, :, :, step] = chosen.astype(BF16).reshape(SIDE, 2, SLOTS, features)

    def select_own(batch, carry):
        select(batch, 0)
        return carry

    lax.fori_loop(0, 2, select_own, 0)

    for batch in range(2):
        for way in range(2):
            rows = pl.ds(way * HALF, HALF)
            got(gathered.at[batch, 1 + 2 * way, rows], g_recv.at[batch, 2 * way, way])
            hand_on(batch, way).start()
            rows = pl.ds((1 - way) * HALF, HALF)
            got(gathered.at[batch, 1 + 2 * way, rows], g_recv.at[batch, 2 * way, 1 - way])
            got(meta.at[batch, 1 + 2 * way], m_recv.at[batch, 2 * way])

    def select_near(piece, carry):
        select(piece % 2, 1 + 2 * (piece // 2))
        return carry

    lax.fori_loop(0, 4, select_near, 0)

    def exchange(batch, step, other):
        if step == 2:
            return remote(
                picked.at[batch, 2, other], passed.at[batch, other], b_send.at[batch, 2, other], f_recv.at[batch, other],
                along(batch, 0, 1 - 2 * other, 0),
            )
        return remote(
            picked.at[batch, step, other], rows_in.at[batch, step, other], b_send.at[batch, step, other],
            b_recv.at[batch, step, other], along(batch, 0, step, other),
        )

    def pass_on(batch, other):
        return remote(
            passed.at[batch, other], rows_in.at[batch, 2, other], f_send.at[batch, other], b_recv.at[batch, 2, other],
            along(batch, 0, 1 - 2 * other, other),
        )

    order = [(2, 0), (2, 1), (1, 0), (3, 0), (1, 1), (3, 1), (0, 1)]

    def select_far(batch, carry):
        for way in range(2):
            got(gathered.at[batch, 2, pl.ds(way * HALF, HALF)], g_recv.at[batch, 1, way])
        got(meta.at[batch, 2], m_recv.at[batch, 1])
        select(batch, 2)
        for step, other in order:
            exchange(batch, step, other).start()
        pltpu.make_async_copy(picked.at[batch, 0, 0], rows_in.at[batch, 0, 0], b_recv.at[batch, 0, 0]).start()
        return carry

    lax.fori_loop(0, 2, select_far, 0)

    for load in loads[1:]:
        load.wait()

    def back(batch, step, other):
        return remote(
            rows_out.at[batch, step, other], returned.at[batch, step, other], o_send.at[batch, step, other],
            o_recv.at[batch, step, other], along(batch, 0, 4 - step, other),
        )

    def back_far(batch, other):
        return remote(
            rows_out.at[batch, 2, other], passed_back.at[batch, other], o_send.at[batch, 2, other],
            p_recv.at[batch, other], along(batch, 0, 2 * other - 1, 0),
        )

    def pass_back(batch, other):
        return remote(
            passed_back.at[batch, other], returned.at[batch, 2, other], p_send.at[batch, other],
            o_recv.at[batch, 2, other], along(batch, 0, 2 * other - 1, other),
        )

    def work(piece, carry):
        batch, turn = piece % 2, piece // 2
        step = turn + turn // 2 - 2 * (turn // 3)

        @pl.when(piece == 2)
        def _():
            for one in range(2):
                for other in range(2):
                    got(passed.at[one, other], f_recv.at[one, other])
                    pass_on(one, other).start()

        got(rows_in.at[batch, step, 0], b_recv.at[batch, step, 0])
        got(rows_in.at[batch, step, 1], b_recv.at[batch, step, 1])
        rows = rows_in[batch, step].reshape(2 * SIDE * SLOTS, features)
        gate_part = jnp.dot(rows, vg[...], preferred_element_type=F32)
        up_part = jnp.dot(rows, vu[...], preferred_element_type=F32)
        hidden = (gate_part / (1.0 + jnp.exp(-gate_part)) * up_part).astype(BF16)
        produced = jnp.dot(hidden, vd[...], preferred_element_type=F32).astype(BF16)
        rows_out[batch, step] = produced.reshape(2, SIDE, SLOTS, features)

        @pl.when(step == 0)
        def _():
            pltpu.make_async_copy(rows_out.at[batch, 0, 0], returned.at[batch, 0, 0], o_recv.at[batch, 0, 0]).start()
            back(batch, 0, 1).start()

        @pl.when(step % 2 == 1)
        def _():
            back(batch, step, 0).start()
            back(batch, step, 1).start()

        @pl.when(step == 2)
        def _():
            back_far(batch, 0).start()
            back_far(batch, 1).start()

        return carry

    lax.fori_loop(0, 8, work, 0)

    for batch in range(2):
        for other in range(2):
            got(passed_back.at[batch, other], p_recv.at[batch, other])
            pass_back(batch, other).start()

    def add_up(batch, step):
        rows = returned[batch, :, :, step].reshape(PICKS, features)
        both = jnp.dot(weigh[batch, step], rows, preferred_element_type=F32)
        return both[:BLOCK] + both[BLOCK:]

    def sum_half(batch, way):
        rows = pl.ds(way * HALF, HALF)
        return remote(
            parts.at[batch, 1, rows], half_in.at[batch, way], h_send.at[batch, way], h_recv.at[batch, way],
            along(batch, 2 * way - 1, 0, 0),
        )

    def sum_home(batch, way):
        return remote(
            parts.at[batch, 2 * way], part_in.at[batch, way], q_send.at[batch, way], q_recv.at[batch, way],
            along(batch, 2 * way - 1, 0, 0),
        )

    def add_far(batch, carry):
        for step in range(SIDE):
            for other in range(2):
                got(returned.at[batch, step, other], o_recv.at[batch, step, other])
        parts[batch, 1] = add_up(batch, 2).astype(BF16)
        sum_half(batch, 0).start()
        sum_half(batch, 1).start()
        return carry

    lax.fori_loop(0, 2, add_far, 0)

    def add_near(batch, carry):
        total[batch] = add_up(batch, 0) + arrived[batch].astype(F32)
        for way in range(2):
            near = add_up(batch, 1 + 2 * way)
            got(half_in.at[batch, way], h_recv.at[batch, way])
            held = half_in[batch, way].astype(F32)
            if way == 0:
                parts[batch, 0, :HALF] = (near[:HALF] + held).astype(BF16)
                parts[batch, 0, HALF:] = near[HALF:].astype(BF16)
            else:
                parts[batch, 2, :HALF] = near[:HALF].astype(BF16)
                parts[batch, 2, HALF:] = (near[HALF:] + held).astype(BF16)
            sum_home(batch, way).start()
        return carry

    lax.fori_loop(0, 2, add_near, 0)

    def finish(batch, carry):
        got(part_in.at[batch, 0], q_recv.at[batch, 0])
        got(part_in.at[batch, 1], q_recv.at[batch, 1])
        final = total[batch] + part_in[batch, 0].astype(F32) + part_in[batch, 1].astype(F32)
        out[batch] = final.astype(BF16)
        return carry

    lax.fori_loop(0, 2, finish, 0)

    for piece in range(4):
        shift(piece).wait_send()
    for batch in range(2):
        for step in (1, 2, 3):
            tell(batch, step).wait_send()
        for way in range(2):
            spread(batch, 0, way).wait_send()
            spread(batch, 1, way).wait_send()
            hand_on(batch, way).wait_send()
            pass_on(batch, way).wait_send()
            pass_back(batch, way).wait_send()
            sum_half(batch, way).wait_send()
            sum_home(batch, way).wait_send()
            back_far(batch, way).wait_send()
        for step, other in order:
            exchange(batch, step, other).wait_send()
        for step, other in ((1, 0), (1, 1), (3, 0), (3, 1), (0, 1)):
            back(batch, step, other).wait_send()


def shards(emitted, levels, expert_ids, gate_values, w_gate, w_up, w_down, w_mod):
    batches, rows, features = emitted.shape[1:]
    top, inner = expert_ids.shape[3], w_gate.shape[3]
    tokens = batches * rows
    embed = level_embedding(levels.reshape(tokens), w_mod.shape[1])
    ids = expert_ids.reshape(tokens, top).T
    gates = gate_values.reshape(tokens, top).T
    anywhere, vmem = pl.BlockSpec(memory_space=pl.ANY), pl.BlockSpec(memory_space=pltpu.VMEM)
    dma = pltpu.SemaphoreType.DMA
    out = pl.pallas_call(
        functools.partial(layer_kernel, lax.axis_size("section"), top),
        out_shape=jax.ShapeDtypeStruct((batches, rows, features), BF16),
        in_specs=[anywhere, vmem, vmem, vmem, anywhere, anywhere, anywhere, anywhere],
        out_specs=vmem,
        scratch_shapes=[
            pltpu.VMEM((features, inner), BF16),
            pltpu.VMEM((features, inner), BF16),
            pltpu.VMEM((inner, features), BF16),
            pltpu.VMEM(w_mod.shape[1:], BF16),
            pltpu.VMEM((tokens, 2 * features), F32),
            pltpu.VMEM((2, SIDE, 16, 2 * BLOCK), F32),
            pltpu.VMEM((2, SIDE, 2 * BLOCK, PICKS), BF16),
            pltpu.VMEM((2, BLOCK, features), BF16),
            pltpu.VMEM((2, SIDE, BLOCK, features), BF16),
            pltpu.VMEM((2, SIDE, 2, SIDE, SLOTS, features), BF16),
            pltpu.VMEM((2, 2, SIDE, SLOTS, features), BF16),
            pltpu.VMEM((2, SIDE, 2, SIDE, SLOTS, features), BF16),
            pltpu.VMEM((2, SIDE, 2, SIDE, SLOTS, features), BF16),
            pltpu.VMEM((2, 2, SIDE, SLOTS, features), BF16),
            pltpu.VMEM((2, SIDE, 2, SIDE, SLOTS, features), BF16),
            pltpu.VMEM((2, 3, BLOCK, features), BF16),
            pltpu.VMEM((2, 2, HALF, features), BF16),
            pltpu.VMEM((2, 2, BLOCK, features), BF16),
            pltpu.VMEM((2, BLOCK, features), F32),
            dma((4,)), dma((4,)), dma((4,)),
            dma((2, 3)), dma((2, 3)),
            dma((2, 2, 2)), dma((2, 3, 2)), dma((2, 2)),
            dma((2, SIDE, 2)), dma((2, SIDE, 2)), dma((2, 2)), dma((2, 2)),
            dma((2, SIDE, 2)), dma((2, SIDE, 2)), dma((2, 2)), dma((2, 2)),
            dma((2, 2)), dma((2, 2)), dma((2, 2)), dma((2, 2)),
        ],
        compiler_params=pltpu.CompilerParams(
            collective_id=0, has_side_effects=True, vmem_limit_bytes=60 * 1024 * 1024
        ),
    )(emitted, embed, ids, gates, w_gate, w_up, w_down, w_mod)
    return out[None]


def solution(mesh):
    placed = (
        P("section", None, "expert", None),
        P("section", None, "expert"),
        P("section", None, "expert", None),
        P("section", None, "expert", None),
        P("section", "expert", None, None),
        P("section", "expert", None, None),
        P("section", "expert", None, None),
        P("section", None, None),
    )
    return jax.shard_map(
        shards,
        mesh=mesh,
        in_specs=placed,
        out_specs=P("section", None, "expert", None),
        check_vma=False,
    )
```

profile of v0, /device:TPU:8, one launch (start us, length us, event | category | flops | bytes accessed | tf_op | source)
XLA Modules:
  0.0 101.0 jit_solution(14369731330568947972)
XLA Ops:
  0.0 0.7 convert_element_type.11
  0.7 0.1 convert_element_type.12
  0.8 1.3 %reshape.18 = s32[128,6]{0,1:T(8,128)} reshape(s32[1,2,64,6]{2,1,3,0:T(2,128)} %param.10) | data formatting | bytes 6144 | tf_op jit(solution)/shard_map/reshape | solution.py:384
  2.1 1.4 %reshape.19 = f32[128,6]{0,1:T(8,128)} reshape(f32[1,2,64,6]{2,1,3,0:T(2,128)} %param.11) | data formatting | bytes 6144 | tf_op jit(solution)/shard_map/reshape | solution.py:385
  3.5 0.3 fusion
  3.8 0.6 pad_maximum_fusion.embed
  4.4 94.7 %shard_map.82 = bf16[2,64,2048]{2,1,0:T(8,128)(2,1)} custom-call(bf16[1,2,64,2048]{3,2,1,0:T(8,128)(2,1)} %emitted.1, bf16[128,256]{1,0:T(8,128)(2,1)} %pad_maximum_fusion.embed, s32[6,128]{1,0:T(8,128)} %bitcast.8, f32[6,128]{1,0:T(8,128)} %bitcast.9, bf16[1,1,2048,768]{3,2,1,0:T(8,128)(2,1)} %w_gate.1, bf16[1,1,2048,768]{3,2,1,0:T(8,128)(2,1)} %w_up.1, ...), custom_call_target="tpu_custom_call" | custom-call | tf_op jit(solution)/shard_map/pallas_call | solution.py:388
  99.2 1.9 %copy.10 = bf16[1,2,64,2048]{3,2,1,0:T(8,128)(2,1)} copy(bf16[1,2,64,2048]{3,2,1,0:T(8,128)(2,1)} %bitcast.7) | data formatting | bytes 1048576
  (1 shorter events, 0.0 us)
where the time goes:
time: 102 us; the launch traced here: 101 us
  Pallas kernels  94.7 us (93%)
  local copies, waits for them, and re-layouts  4.68 us (5%)
  other arithmetic  1.64 us (2%)
    pallas_call x1, Pallas kernels, shards(): pl.pallas_call(functools.partial(layer_kernel, lax.axis_size('section'),...  94.7 us

commit v1 on v0

v1 whole, which is shorter than its diff:
```python
import functools
import math

import jax
import jax.numpy as jnp
from jax import lax
from jax.experimental import pallas as pl
from jax.experimental.pallas import tpu as pltpu
from jax.sharding import PartitionSpec as P

epsilon = 1e-06
MESH = pl.DeviceIdType.MESH
F32, BF16 = jnp.float32, jnp.bfloat16
SIDE = 4
SLOTS = 16
BLOCK = 64
HALF = BLOCK // 2
PIECE = BLOCK // 4
OFFSET = (0, 1, 3, 2)
PICKS = SIDE * 2 * SLOTS


def layer_kernel(
    sections, top,
    emitted, levels, ids, gates, w_gate, w_up, w_down, w_mod,
    out,
    vg, vu, vd, vm, vl, vi, vw, mod, meta, weigh,
    arrived, gathered, picked, passed, rows_in, rows_out, passed_back, returned,
    far_part, near_part, near_held, half_in, part_in, total,
    load_sem, z_send, z_recv, m_send, m_recv, g_send, g_recv, gf_send, gf_recv,
    b_send, b_recv, f_recv, f_send, o_send, o_recv, p_recv, p_send, h_send, h_recv, q_send, q_recv,
):
    section = lax.axis_index("section")
    place = lax.axis_index("expert")
    x, y, core = place // 8, (place // 2) % SIDE, place % 2
    features = arrived.shape[2]

    def at(dx, dy, other):
        seat = core + other * (1 - 2 * core)
        return (section, ((x + dx + 8) % SIDE) * 8 + ((y + dy + 8) % SIDE) * 2 + seat)

    def along(batch, da, db, other):
        return at(da + batch * (db - da), db + batch * (da - db), other)

    def remote(src, dst, send, recv, device):
        return pltpu.make_async_remote_copy(
            src_ref=src, dst_ref=dst, send_sem=send, recv_sem=recv, device_id=device, device_id_type=MESH
        )

    def got(dst, recv):
        remote(dst, dst, recv, recv, (section, place)).wait_recv()

    def left(src, send):
        remote(src, src, send, send, (section, place)).wait_send()

    after = ((section + 1) % sections, place)
    ahead = ((section + sections - 1) % sections, place)

    barrier = pltpu.get_barrier_semaphore()
    friends = [after, ahead, at(0, 0, 1), at(2, 0, 0), at(0, 2, 0)]
    for step in (1, -1):
        for other in (0, 1):
            friends += [at(step, 0, other), at(0, step, other)]
    for friend in friends:
        pl.semaphore_signal(barrier, inc=1, device_id=friend, device_id_type=MESH)

    sources = (levels.at[0], ids.at[0], gates.at[0], w_mod.at[0], w_gate.at[0, 0], w_up.at[0, 0], w_down.at[0, 0])
    targets = (vl, vi, vw, vm, vg, vu, vd)
    loads = [pltpu.make_async_copy(a, b, load_sem.at[i]) for i, (a, b) in enumerate(zip(sources, targets))]
    for load in loads[:4]:
        load.start()
    pl.semaphore_wait(barrier, len(friends))

    def shift(piece):
        batch, rows = piece % 2, pl.ds((piece // 2) * PIECE, PIECE)
        return remote(
            emitted.at[0, batch, rows], arrived.at[batch, rows], z_send.at[piece], z_recv.at[piece], after
        )

    for piece in range(8):
        shift(piece).start()
    for load in loads[4:]:
        load.start()

    for load in loads[:3]:
        load.wait()

    experts = SIDE * SIDE * 2
    name = lax.broadcasted_iota(jnp.int32, (experts, BLOCK), 0)
    row = lax.broadcasted_iota(jnp.int32, (BLOCK, BLOCK), 0)
    col = lax.broadcasted_iota(jnp.int32, (BLOCK, BLOCK), 1)
    earlier = jnp.where(row < col, 1.0, 0.0).astype(BF16)
    for batch in range(2):
        meta[batch, 0] = jnp.full((16, 2 * BLOCK), -1.0, F32)
        numbers = [vi[k, batch : batch + 1, :] for k in range(top)]
        named = jnp.zeros((experts, BLOCK), F32)
        for number in numbers:
            named = named + jnp.where(number == name, 1.0, 0.0)
        before = jnp.dot(named.astype(BF16), earlier, preferred_element_type=F32)
        for k, number in enumerate(numbers):
            slot = jnp.sum(jnp.where(number == name, before, 0.0), axis=0, keepdims=True)
            meta[batch, 0, k : k + 1, :BLOCK] = number.astype(F32) * SLOTS + slot
            meta[batch, 0, 8 + k : 9 + k, :BLOCK] = vw[k, batch : batch + 1, :]

    entries = w_mod.shape[1] // 2
    level = jnp.concatenate([vl[0:1, :], vl[1:2, :]], axis=1).astype(F32)
    level = jnp.broadcast_to(level, (2 * BLOCK, 2 * BLOCK)).T
    index = lax.broadcasted_iota(jnp.int32, (1, entries), 1).astype(F32)
    angles = level * jnp.exp(-math.log(10000.0) * index / entries)
    embed = jnp.concatenate([jnp.cos(angles), jnp.sin(angles)], axis=1).astype(BF16)
    loads[3].wait()
    mod[...] = jnp.dot(embed, vm[...], preferred_element_type=F32)

    def tell(batch, p):
        return remote(
            meta.at[batch, 0], meta.at[batch, p], m_send.at[batch, p - 1], m_recv.at[batch, p - 1],
            along(batch, OFFSET[p], 0, 0),
        )

    for batch in range(2):
        for p in (1, 2, 3):
            tell(batch, p).start()

    def spread(batch, part, way):
        rows = pl.ds(part * PIECE, PIECE)
        return remote(
            gathered.at[batch, 0, rows], gathered.at[batch, 1 + way, rows],
            g_send.at[batch, way, part], g_recv.at[batch, way, part], along(batch, 1 - 2 * way, 0, 0),
        )

    def normalize(batch, part):
        rows = pl.ds(part * PIECE, PIECE)
        got(arrived.at[batch, rows], z_recv.at[batch + 2 * part])
        values = arrived[batch, rows, :].astype(F32)
        mean_square = jnp.mean(values * values, axis=1, keepdims=True)
        own = pl.ds(batch * BLOCK + part * PIECE, PIECE)
        normed = values * lax.rsqrt(mean_square + epsilon) * (1.0 + mod[own, :features]) + mod[own, features:]
        gathered[batch, 0, rows, :] = normed.astype(BF16)
        spread(batch, part, 0).start()
        spread(batch, part, 1).start()

    def spread_in(batch, way, half):
        for part in (2 * half, 2 * half + 1):
            got(gathered.at[batch, 1 + way, pl.ds(part * PIECE, PIECE)], g_recv.at[batch, way, part])

    def hand_on(batch, way):
        rows = pl.ds(way * HALF, HALF)
        return remote(
            gathered.at[batch, 1 + way, rows], gathered.at[batch, 3, rows],
            gf_send.at[batch, way], gf_recv.at[batch, way], along(batch, 1 - 2 * way, 0, 0),
        )

    def forward(batch, way):
        spread_in(batch, way, way)
        hand_on(batch, way).start()

    pick = lax.broadcasted_iota(jnp.int32, (PICKS, 2 * BLOCK), 0)
    far, other_seat, slot_of = pick // (2 * SLOTS), (pick // SLOTS) % 2, pick % SLOTS
    seat_of = core + other_seat * (1 - 2 * core)
    wanted = []
    for batch in range(2):
        if batch == 0:
            line = x * 8 + ((y + far) % SIDE) * 2
        else:
            line = ((x + far) % SIDE) * 8 + y * 2
        wanted.append(((line + seat_of) * SLOTS + slot_of).astype(F32))

    def exchange(p, batch, block):
        step, other = block // 2, block % 2
        if step == 2:
            return remote(
                picked.at[p, batch, block], passed.at[p, batch, other], b_send.at[p, batch], f_recv.at[p, batch],
                along(batch, 0, 1 - 2 * other, 0),
            )
        return remote(
            picked.at[p, batch, block], rows_in.at[p, batch, block], b_send.at[p, batch], b_recv.at[p, batch],
            along(batch, 0, step, other),
        )

    order = (4, 5, 2, 6, 3, 7, 1)

    def select(batch, p):
        if p == 3:
            for way in range(2):
                got(gathered.at[batch, 3, pl.ds(way * HALF, HALF)], gf_recv.at[batch, way])
        elif p:
            spread_in(batch, p - 1, 2 - p)
        if p:
            got(meta.at[batch, p], m_recv.at[batch, p - 1])
        hit = jnp.zeros((PICKS, 2 * BLOCK), F32)
        worth = jnp.zeros((PICKS, 2 * BLOCK), F32)
        for k in range(top):
            same = meta[batch, p, k : k + 1, :] == wanted[batch]
            hit = jnp.where(same, 1.0, hit)
            worth = jnp.where(same, meta[batch, p, 8 + k : 9 + k, :], worth)
        chosen = jnp.dot(hit[:, :BLOCK].astype(BF16), gathered[batch, p], preferred_element_type=F32)
        chosen = chosen.astype(BF16).reshape(2 * SIDE, SLOTS, features)
        picked[p, batch] = chosen
        rows_in[p, batch, 0] = chosen[0]
        for block in order:
            exchange(p, batch, block).start()
        worth = worth.T
        high = worth[:BLOCK].astype(BF16)
        weigh[batch, p, :BLOCK, :] = high
        weigh[batch, p, BLOCK:, :] = (worth[:BLOCK] - high.astype(F32)).astype(BF16)

    def pass_on(p, batch):
        return [
            remote(
                passed.at[p, batch, other], rows_in.at[p, batch, 4 + other], f_send.at[p, batch], b_recv.at[p, batch],
                along(batch, 0, 1 - 2 * other, other),
            )
            for other in range(2)
        ]

    def move_on(p, batch):
        got(passed.at[p, batch], f_recv.at[p, batch])
        for copy in pass_on(p, batch):
            copy.start()

    for part in (0, 1):
        for batch in range(2):
            normalize(batch, part)
    normalize(0, 2)
    forward(0, 0)
    normalize(1, 2)
    forward(1, 0)
    normalize(0, 3)
    select(0, 0)
    normalize(1, 3)
    select(1, 0)
    forward(0, 1)
    forward(1, 1)
    move_on(0, 0)
    move_on(0, 1)
    select(0, 1)
    select(1, 1)
    select(0, 2)
    select(1, 2)
    move_on(1, 0)
    move_on(1, 1)
    select(0, 3)
    select(1, 3)
    move_on(2, 0)
    move_on(2, 1)

    for load in loads[4:]:
        load.wait()

    def back(p, batch, block):
        step, other = block // 2, block % 2
        if step == 2:
            return remote(
                rows_out.at[p, batch, block], passed_back.at[p, batch, other], o_send.at[p, batch],
                p_recv.at[p, batch], along(batch, 0, 2 * other - 1, 0),
            )
        return remote(
            rows_out.at[p, batch, block], returned.at[p, batch, block], o_send.at[p, batch], o_recv.at[p, batch],
            along(batch, 0, 4 - step, other),
        )

    def pass_back(p, batch):
        return [
            remote(
                passed_back.at[p, batch, other], returned.at[p, batch, 4 + other], p_send.at[p, batch],
                o_recv.at[p, batch], along(batch, 0, 2 * other - 1, other),
            )
            for other in range(2)
        ]

    def move_back(p):
        for batch in range(2):
            got(passed_back.at[p, batch], p_recv.at[p, batch])
            for copy in pass_back(p, batch):
                copy.start()

    def send_back(p):
        for block in order:
            for batch in range(2):
                back(p, batch, block).start()

    def work(p, carry):
        @pl.when(p == 1)
        def _():
            move_on(3, 0)
            move_on(3, 1)

        for batch in range(2):
            got(rows_in.at[p, batch, pl.ds(1, 7)], b_recv.at[p, batch])
        rows = rows_in[p].reshape(2 * PICKS, features)
        gate_part = jnp.dot(rows, vg[...], preferred_element_type=F32)
        up_part = jnp.dot(rows, vu[...], preferred_element_type=F32)
        hidden = (gate_part / (1.0 + jnp.exp(-gate_part)) * up_part).astype(BF16)
        produced = jnp.dot(hidden, vd[...], preferred_element_type=F32).astype(BF16)
        produced = produced.reshape(2, 2 * SIDE, SLOTS, features)
        rows_out[p] = produced
        for batch in range(2):
            returned[p, batch, 0] = produced[batch, 0]

        @pl.when(p > 1)
        def _():
            move_back(p - 1)

        @pl.when(p > 0)
        def _():
            send_back(p)

        return carry

    lax.fori_loop(0, SIDE, work, 0)

    def add_up(p, batch):
        got(returned.at[p, batch, pl.ds(1, 7)], o_recv.at[p, batch])
        rows = returned[p, batch].reshape(PICKS, features)
        both = jnp.dot(weigh[batch, p], rows, preferred_element_type=F32)
        return both[:BLOCK] + both[BLOCK:]

    def sum_half(batch, way):
        return remote(
            far_part.at[batch, way], half_in.at[batch, way], h_send.at[batch, way], h_recv.at[batch, way],
            along(batch, 2 * way - 1, 0, 0),
        )

    def sum_home(batch, way, part):
        return remote(
            near_part.at[batch, way, part], part_in.at[batch, way, part], q_send.at[batch, way, part],
            q_recv.at[batch, way, part], along(batch, 2 * way - 1, 0, 0),
        )

    def add_own(batch, carry):
        total[batch] = add_up(0, batch) + arrived[batch].astype(F32)
        return carry

    def add_near(way):
        def add(batch, carry):
            near = add_up(1 + way, batch).reshape(2, HALF, features)
            near_held[batch, way] = near[way]
            near_part[batch, way, 1 - way] = near[1 - way].astype(BF16)
            sum_home(batch, way, 1 - way).start()
            return carry

        return add

    def add_far(batch, carry):
        far_part[batch] = add_up(3, batch).astype(BF16).reshape(2, HALF, features)
        sum_half(batch, 0).start()
        sum_half(batch, 1).start()
        return carry

    lax.fori_loop(0, 2, add_near(0), 0)
    move_back(3)
    send_back(0)
    lax.fori_loop(0, 2, add_near(1), 0)
    lax.fori_loop(0, 2, add_far, 0)
    move_back(0)

    def add_half(batch, carry):
        for way in range(2):
            got(half_in.at[batch, way], h_recv.at[batch, way])
            near_part[batch, way, way] = (near_held[batch, way] + half_in[batch, way].astype(F32)).astype(BF16)
            sum_home(batch, way, way).start()
        return carry

    lax.fori_loop(0, 2, add_half, 0)
    lax.fori_loop(0, 2, add_own, 0)

    def finish(batch, carry):
        for part in range(2):
            for way in range(2):
                got(part_in.at[batch, way, part], q_recv.at[batch, way, part])
            rows = pl.ds(part * HALF, HALF)
            sums = part_in[batch, 0, part].astype(F32) + part_in[batch, 1, part].astype(F32)
            out[batch, rows, :] = (total[batch, rows, :] + sums).astype(BF16)
        return carry

    lax.fori_loop(0, 2, finish, 0)

    for piece in range(8):
        shift(piece).wait_send()
    for batch in range(2):
        for p in (1, 2, 3):
            tell(batch, p).wait_send()
        for way in range(2):
            for part in range(4):
                spread(batch, part, way).wait_send()
            hand_on(batch, way).wait_send()
            sum_half(batch, way).wait_send()
            sum_home(batch, way, 0).wait_send()
            sum_home(batch, way, 1).wait_send()
        for p in range(SIDE):
            left(picked.at[p, batch, pl.ds(1, 7)], b_send.at[p, batch])
            left(passed.at[p, batch], f_send.at[p, batch])
            left(rows_out.at[p, batch, pl.ds(1, 7)], o_send.at[p, batch])
            left(passed_back.at[p, batch], p_send.at[p, batch])


def shards(emitted, levels, expert_ids, gate_values, w_gate, w_up, w_down, w_mod):
    batches, rows, features = emitted.shape[1:]
    top, inner = expert_ids.shape[3], w_gate.shape[3]
    tokens = batches * rows
    ids = expert_ids.transpose(0, 3, 1, 2)
    gates = gate_values.transpose(0, 3, 1, 2)
    anywhere, vmem = pl.BlockSpec(memory_space=pl.ANY), pl.BlockSpec(memory_space=pltpu.VMEM)
    dma = pltpu.SemaphoreType.DMA
    lines = pltpu.VMEM((SIDE, 2, 2 * SIDE, SLOTS, features), BF16)
    out = pl.pallas_call(
        functools.partial(layer_kernel, lax.axis_size("section"), top),
        out_shape=jax.ShapeDtypeStruct((batches, rows, features), BF16),
        in_specs=[anywhere] * 8,
        out_specs=vmem,
        scratch_shapes=[
            pltpu.VMEM((features, inner), BF16),
            pltpu.VMEM((features, inner), BF16),
            pltpu.VMEM((inner, features), BF16),
            pltpu.VMEM(w_mod.shape[1:], BF16),
            pltpu.VMEM((batches, rows), jnp.int32),
            pltpu.VMEM((top, batches, rows), jnp.int32),
            pltpu.VMEM((top, batches, rows), F32),
            pltpu.VMEM((tokens, 2 * features), F32),
            pltpu.VMEM((2, SIDE, 16, 2 * BLOCK), F32),
            pltpu.VMEM((2, SIDE, 2 * BLOCK, PICKS), BF16),
            pltpu.VMEM((2, BLOCK, features), BF16),
            pltpu.VMEM((2, SIDE, BLOCK, features), BF16),
            lines,
            pltpu.VMEM((SIDE, 2, 2, SLOTS, features), BF16),
            lines,
            lines,
            pltpu.VMEM((SIDE, 2, 2, SLOTS, features), BF16),
            lines,
            pltpu.VMEM((2, 2, HALF, features), BF16),
            pltpu.VMEM((2, 2, 2, HALF, features), BF16),
            pltpu.VMEM((2, 2, HALF, features), F32),
            pltpu.VMEM((2, 2, HALF, features), BF16),
            pltpu.VMEM((2, 2, 2, HALF, features), BF16),
            pltpu.VMEM((2, BLOCK, features), F32),
            dma((7,)), dma((8,)), dma((8,)),
            dma((2, 3)), dma((2, 3)),
            dma((2, 2, 4)), dma((2, 2, 4)), dma((2, 2)), dma((2, 2)),
            dma((SIDE, 2)), dma((SIDE, 2)), dma((SIDE, 2)), dma((SIDE, 2)),
            dma((SIDE, 2)), dma((SIDE, 2)), dma((SIDE, 2)), dma((SIDE, 2)),
            dma((2, 2)), dma((2, 2)), dma((2, 2, 2)), dma((2, 2, 2)),
        ],
        compiler_params=pltpu.CompilerParams(
            collective_id=0, has_side_effects=True, vmem_limit_bytes=60 * 1024 * 1024
        ),
    )(emitted, levels, ids, gates, w_gate, w_up, w_down, w_mod)
    return out[None]


def solution(mesh):
    placed = (
        P("section", None, "expert", None),
        P("section", None, "expert"),
        P("section", None, "expert", None),
        P("section", None, "expert", None),
        P("section", "expert", None, None),
        P("section", "expert", None, None),
        P("section", "expert", None, None),
        P("section", None, None),
    )
    return jax.shard_map(
        shards,
        mesh=mesh,
        in_specs=placed,
        out_specs=P("section", None, "expert", None),
        check_vma=False,
    )
```

time: 102 us -> 88 us (0.86)
  Pallas kernels: 94.7 us -> 86 us
  local copies, waits for them, and re-layouts: 4.68 us -> 1.88 us
  other arithmetic: 1.64 us -> 0 us
    pallas_call x1, Pallas kernels: 94.7 us -> 86 us  [shards(): pl.pallas_call(functools.partial(layer_kernel, lax.axis_size('section'),...]
    reshape x2 -> x0, local copies, waits for them, and re-layouts: 2.71 us -> none  [the longest x1 1.36 us: shards(): gates = gate_values.reshape(tokens, top).T]
where the time goes in v1:
time: 88 us; the launch traced here: 87.9 us
  Pallas kernels  86 us (98%)
  local copies, waits for them, and re-layouts  1.88 us (2%)
    pallas_call x1, Pallas kernels, shards(): pl.pallas_call(functools.partial(layer_kernel, lax.axis_size('section'),...  86 us
    unnamed x1, local copies, waits for them, and re-layouts  1.88 us

profile of v1, /device:TPU:8, one launch (start us, length us, event | category | flops | bytes accessed | tf_op | source)
XLA Modules:
  0.0 87.9 jit_solution(6895690307418541852)
XLA Ops:
  0.0 86.0 %shard_map.82 = bf16[2,64,2048]{2,1,0:T(8,128)(2,1)} custom-call(bf16[1,2,64,2048]{3,2,1,0:T(8,128)(2,1)} %emitted.1, s32[1,2,64]{2,1,0:T(2,128)} %levels.1, s32[1,6,2,64]{3,2,1,0:T(2,128)} %bitcast.4, f32[1,6,2,64]{3,2,1,0:T(2,128)} %bitcast.5, bf16[1,1,2048,768]{3,2,1,0:T(8,128)(2,1)} %w_gate.1, bf16[1,1,2048,768]{3,2,1,0:T(8,128)(2,1)} %w_up.1, ...), custom_call_target="tpu_custom_call" | custom-call | tf_op jit(solution)/shard_map/pallas_call | solution.py:406
  86.0 1.9 %copy.10 = bf16[1,2,64,2048]{3,2,1,0:T(8,128)(2,1)} copy(bf16[1,2,64,2048]{3,2,1,0:T(8,128)(2,1)} %bitcast.3) | data formatting | bytes 1048576

commit v2 on v1

--- a/solution.py
+++ b/solution.py
@@ -226,8 +226,8 @@
     normalize(1, 2)
     forward(1, 0)
     normalize(0, 3)
+    normalize(1, 3)
     select(0, 0)
-    normalize(1, 3)
     select(1, 0)
     forward(0, 1)
     forward(1, 1)
@@ -403,6 +403,10 @@
     anywhere, vmem = pl.BlockSpec(memory_space=pl.ANY), pl.BlockSpec(memory_space=pltpu.VMEM)
     dma = pltpu.SemaphoreType.DMA
     lines = pltpu.VMEM((SIDE, 2, 2 * SIDE, SLOTS, features), BF16)
+    held = [
+        pltpu.with_memory_space_constraint(array, pltpu.HBM)
+        for array in (emitted, levels, ids, gates, w_gate, w_up, w_down, w_mod)
+    ]
     out = pl.pallas_call(
         functools.partial(layer_kernel, lax.axis_size("section"), top),
         out_shape=jax.ShapeDtypeStruct((batches, rows, features), BF16),
@@ -441,9 +445,9 @@
             dma((2, 2)), dma((2, 2)), dma((2, 2, 2)), dma((2, 2, 2)),
         ],
         compiler_params=pltpu.CompilerParams(
-            collective_id=0, has_side_effects=True, vmem_limit_bytes=60 * 1024 * 1024
+            collective_id=0, has_side_effects=True, vmem_limit_bytes=52 * 1024 * 1024
         ),
-    )(emitted, levels, ids, gates, w_gate, w_up, w_down, w_mod)
+    )(*held)
     return out[None]
 
 

time: 88 us -> 85.2 us (0.968)
  Pallas kernels: 86 us -> 83.8 us
  local copies, waits for them, and re-layouts: 1.88 us -> 0.8 us
    pallas_call x1, Pallas kernels: 86 us -> 83.8 us  [shards(): pl.pallas_call(functools.partial(layer_kernel, lax.axis_size('section'),...]
    unnamed x1, local copies, waits for them, and re-layouts: 1.88 us -> 0.8 us
where the time goes in v2:
time: 85.2 us; the launch traced here: 84.6 us
  Pallas kernels  83.8 us (98%)
    pallas_call x1, Pallas kernels, shards(): pl.pallas_call(functools.partial(layer_kernel, lax.axis_size('section'),...  83.8 us

profile of v2, /device:TPU:8, one launch (start us, length us, event | category | flops | bytes accessed | tf_op | source)
XLA Modules:
  0.0 84.6 jit_solution(13163671418603281503)
XLA Ops:
  0.0 83.8 %shard_map.82 = bf16[2,64,2048]{2,1,0:T(8,128)(2,1)S(1)} custom-call(bf16[1,2,64,2048]{3,2,1,0:T(8,128)(2,1)} %emitted.1, s32[1,2,64]{2,1,0:T(2,128)} %levels.1, s32[1,6,2,64]{3,2,1,0:T(2,128)} %bitcast.4, f32[1,6,2,64]{3,2,1,0:T(2,128)} %bitcast.5, bf16[1,1,2048,768]{3,2,1,0:T(8,128)(2,1)} %w_gate.1, bf16[1,1,2048,768]{3,2,1,0:T(8,128)(2,1)} %w_up.1, ...), custom_call_target="tpu_custom_call" | custom-call | tf_op jit(solution)/shard_map/pallas_call | solution.py:410
  83.8 0.8 copy.10

commit v3 on v2

--- a/solution.py
+++ b/solution.py
@@ -57,7 +57,7 @@
     ahead = ((section + sections - 1) % sections, place)
 
     barrier = pltpu.get_barrier_semaphore()
-    friends = [after, ahead, at(0, 0, 1), at(2, 0, 0), at(0, 2, 0)]
+    friends = [after, ahead, at(0, 0, 1)]
     for step in (1, -1):
         for other in (0, 1):
             friends += [at(step, 0, other), at(0, step, other)]
@@ -67,8 +67,6 @@
     sources = (levels.at[0], ids.at[0], gates.at[0], w_mod.at[0], w_gate.at[0, 0], w_up.at[0, 0], w_down.at[0, 0])
     targets = (vl, vi, vw, vm, vg, vu, vd)
     loads = [pltpu.make_async_copy(a, b, load_sem.at[i]) for i, (a, b) in enumerate(zip(sources, targets))]
-    for load in loads[:4]:
-        load.start()
     pl.semaphore_wait(barrier, len(friends))
 
     def shift(piece):
@@ -79,7 +77,7 @@
 
     for piece in range(8):
         shift(piece).start()
-    for load in loads[4:]:
+    for load in loads:
         load.start()
 
     for load in loads[:3]:
@@ -113,12 +111,12 @@
 
     def tell(batch, p):
         return remote(
-            meta.at[batch, 0], meta.at[batch, p], m_send.at[batch, p - 1], m_recv.at[batch, p - 1],
-            along(batch, OFFSET[p], 0, 0),
+            meta.at[batch, p // 3], meta.at[batch, p], m_send.at[batch, p - 1], m_recv.at[batch, p - 1],
+            along(batch, OFFSET[p % 3 + p // 3], 0, 0),
         )
 
     for batch in range(2):
-        for p in (1, 2, 3):
+        for p in (1, 2):
             tell(batch, p).start()
 
     def spread(batch, part, way):
@@ -153,6 +151,9 @@
     def forward(batch, way):
         spread_in(batch, way, way)
         hand_on(batch, way).start()
+        if way == 0:
+            got(meta.at[batch, 1], m_recv.at[batch, 0])
+            tell(batch, 3).start()
 
     pick = lax.broadcasted_iota(jnp.int32, (PICKS, 2 * BLOCK), 0)
     far, other_seat, slot_of = pick // (2 * SLOTS), (pick // SLOTS) % 2, pick % SLOTS
@@ -185,7 +186,7 @@
                 got(gathered.at[batch, 3, pl.ds(way * HALF, HALF)], gf_recv.at[batch, way])
         elif p:
             spread_in(batch, p - 1, 2 - p)
-        if p:
+        if p > 1:
             got(meta.at[batch, p], m_recv.at[batch, p - 1])
         hit = jnp.zeros((PICKS, 2 * BLOCK), F32)
         worth = jnp.zeros((PICKS, 2 * BLOCK), F32)
@@ -241,8 +242,6 @@
     move_on(1, 1)
     select(0, 3)
     select(1, 3)
-    move_on(2, 0)
-    move_on(2, 1)
 
     for load in loads[4:]:
         load.wait()
@@ -282,6 +281,8 @@
     def work(p, carry):
         @pl.when(p == 1)
         def _():
+            move_on(2, 0)
+            move_on(2, 1)
             move_on(3, 0)
             move_on(3, 1)
 
@@ -315,10 +316,10 @@
         both = jnp.dot(weigh[batch, p], rows, preferred_element_type=F32)
         return both[:BLOCK] + both[BLOCK:]
 
-    def sum_half(batch, way):
-        return remote(
-            far_part.at[batch, way], half_in.at[batch, way], h_send.at[batch, way], h_recv.at[batch, way],
-            along(batch, 2 * way - 1, 0, 0),
+    def sum_half(batch, way, piece):
+        return remote(
+            far_part.at[batch, way, piece], half_in.at[batch, way, piece], h_send.at[batch, way, piece],
+            h_recv.at[batch, way, piece], along(batch, 2 * way - 1, 0, 0),
         )
 
     def sum_home(batch, way, part):
@@ -333,18 +334,21 @@
 
     def add_near(way):
         def add(batch, carry):
-            near = add_up(1 + way, batch).reshape(2, HALF, features)
-            near_held[batch, way] = near[way]
-            near_part[batch, way, 1 - way] = near[1 - way].astype(BF16)
-            sum_home(batch, way, 1 - way).start()
+            near = add_up(1 + way, batch).reshape(4, PIECE, features)
+            for piece in range(2):
+                part = 2 * (1 - way) + piece
+                near_held[batch, way, piece] = near[2 * way + piece]
+                near_part[batch, way, part] = near[part].astype(BF16)
+                sum_home(batch, way, part).start()
             return carry
 
         return add
 
     def add_far(batch, carry):
-        far_part[batch] = add_up(3, batch).astype(BF16).reshape(2, HALF, features)
-        sum_half(batch, 0).start()
-        sum_half(batch, 1).start()
+        far_part[batch] = add_up(3, batch).astype(BF16).reshape(2, 2, PIECE, features)
+        for piece in range(2):
+            for way in range(2):
+                sum_half(batch, way, piece).start()
         return carry
 
     lax.fori_loop(0, 2, add_near(0), 0)
@@ -354,23 +358,28 @@
     lax.fori_loop(0, 2, add_far, 0)
     move_back(0)
 
-    def add_half(batch, carry):
-        for way in range(2):
-            got(half_in.at[batch, way], h_recv.at[batch, way])
-            near_part[batch, way, way] = (near_held[batch, way] + half_in[batch, way].astype(F32)).astype(BF16)
-            sum_home(batch, way, way).start()
+    def add_half(piece, carry):
+        for batch in range(2):
+            for way in range(2):
+                got(half_in.at[batch, way, piece], h_recv.at[batch, way, piece])
+                part = 2 * way + piece
+                held = near_held[batch, way, piece] + half_in[batch, way, piece].astype(F32)
+                near_part[batch, way, part] = held.astype(BF16)
+                sum_home(batch, way, part).start()
         return carry
 
     lax.fori_loop(0, 2, add_half, 0)
     lax.fori_loop(0, 2, add_own, 0)
 
-    def finish(batch, carry):
-        for part in range(2):
-            for way in range(2):
-                got(part_in.at[batch, way, part], q_recv.at[batch, way, part])
-            rows = pl.ds(part * HALF, HALF)
-            sums = part_in[batch, 0, part].astype(F32) + part_in[batch, 1, part].astype(F32)
-            out[batch, rows, :] = (total[batch, rows, :] + sums).astype(BF16)
+    def finish(piece, carry):
+        for batch in range(2):
+            for half in range(2):
+                part = 2 * half + piece
+                for way in range(2):
+                    got(part_in.at[batch, way, part], q_recv.at[batch, way, part])
+                rows = pl.ds(pl.multiple_of(part * PIECE, PIECE), PIECE)
+                sums = part_in[batch, 0, part].astype(F32) + part_in[batch, 1, part].astype(F32)
+                out[batch, rows, :] = (total[batch, rows, :] + sums).astype(BF16)
         return carry
 
     lax.fori_loop(0, 2, finish, 0)
@@ -384,9 +393,10 @@
             for part in range(4):
                 spread(batch, part, way).wait_send()
             hand_on(batch, way).wait_send()
-            sum_half(batch, way).wait_send()
-            sum_home(batch, way, 0).wait_send()
-            sum_home(batch, way, 1).wait_send()
+            for piece in range(2):
+                sum_half(batch, way, piece).wait_send()
+            for part in range(4):
+                sum_home(batch, way, part).wait_send()
         for p in range(SIDE):
             left(picked.at[p, batch, pl.ds(1, 7)], b_send.at[p, batch])
             left(passed.at[p, batch], f_send.at[p, batch])
@@ -431,18 +441,18 @@
             lines,
             pltpu.VMEM((SIDE, 2, 2, SLOTS, features), BF16),
             lines,
-            pltpu.VMEM((2, 2, HALF, features), BF16),
-            pltpu.VMEM((2, 2, 2, HALF, features), BF16),
-            pltpu.VMEM((2, 2, HALF, features), F32),
-            pltpu.VMEM((2, 2, HALF, features), BF16),
-            pltpu.VMEM((2, 2, 2, HALF, features), BF16),
+            pltpu.VMEM((2, 2, 2, PIECE, features), BF16),
+            pltpu.VMEM((2, 2, 4, PIECE, features), BF16),
+            pltpu.VMEM((2, 2, 2, PIECE, features), F32),
+            pltpu.VMEM((2, 2, 2, PIECE, features), BF16),
+            pltpu.VMEM((2, 2, 4, PIECE, features), BF16),
             pltpu.VMEM((2, BLOCK, features), F32),
             dma((7,)), dma((8,)), dma((8,)),
             dma((2, 3)), dma((2, 3)),
             dma((2, 2, 4)), dma((2, 2, 4)), dma((2, 2)), dma((2, 2)),
             dma((SIDE, 2)), dma((SIDE, 2)), dma((SIDE, 2)), dma((SIDE, 2)),
             dma((SIDE, 2)), dma((SIDE, 2)), dma((SIDE, 2)), dma((SIDE, 2)),
-            dma((2, 2)), dma((2, 2)), dma((2, 2, 2)), dma((2, 2, 2)),
+            dma((2, 2, 2)), dma((2, 2, 2)), dma((2, 2, 4)), dma((2, 2, 4)),
         ],
         compiler_params=pltpu.CompilerParams(
             collective_id=0, has_side_effects=True, vmem_limit_bytes=52 * 1024 * 1024

time: 85.2 us -> 85.6 us (level)
  no operation moved by 1% of the time
where the time goes in v3:
time: 85.6 us; the launch traced here: 85 us
  Pallas kernels  84.2 us (98%)
    pallas_call x1, Pallas kernels, shards(): pl.pallas_call(functools.partial(layer_kernel, lax.axis_size('section'),...  84.2 us

profile of v3, /device:TPU:8, one launch (start us, length us, event | category | flops | bytes accessed | tf_op | source)
XLA Modules:
  0.0 85.0 jit_solution(8489913114519966856)
XLA Ops:
  0.0 84.2 %shard_map.82 = bf16[2,64,2048]{2,1,0:T(8,128)(2,1)S(1)} custom-call(bf16[1,2,64,2048]{3,2,1,0:T(8,128)(2,1)} %emitted.1, s32[1,2,64]{2,1,0:T(2,128)} %levels.1, s32[1,6,2,64]{3,2,1,0:T(2,128)} %bitcast.4, f32[1,6,2,64]{3,2,1,0:T(2,128)} %bitcast.5, bf16[1,1,2048,768]{3,2,1,0:T(8,128)(2,1)} %w_gate.1, bf16[1,1,2048,768]{3,2,1,0:T(8,128)(2,1)} %w_up.1, ...), custom_call_target="tpu_custom_call" | custom-call | tf_op jit(solution)/shard_map/pallas_call | solution.py:420
  84.2 0.8 copy.10

commit v4 on v2

--- a/solution.py
+++ b/solution.py
@@ -241,8 +241,6 @@
     move_on(1, 1)
     select(0, 3)
     select(1, 3)
-    move_on(2, 0)
-    move_on(2, 1)
 
     for load in loads[4:]:
         load.wait()
@@ -282,6 +280,8 @@
     def work(p, carry):
         @pl.when(p == 1)
         def _():
+            move_on(2, 0)
+            move_on(2, 1)
             move_on(3, 0)
             move_on(3, 1)
 

time: 85.2 us -> 85.2 us (level)
  no operation moved by 1% of the time
where the time goes in v4:
time: 85.2 us; the launch traced here: 84.6 us
  Pallas kernels  83.8 us (98%)
    pallas_call x1, Pallas kernels, shards(): pl.pallas_call(functools.partial(layer_kernel, lax.axis_size('section'),...  83.8 us

profile of v4, /device:TPU:8, one launch (start us, length us, event | category | flops | bytes accessed | tf_op | source)
XLA Modules:
  0.0 84.6 jit_solution(4871405434007123418)
XLA Ops:
  0.0 83.8 %shard_map.82 = bf16[2,64,2048]{2,1,0:T(8,128)(2,1)S(1)} custom-call(bf16[1,2,64,2048]{3,2,1,0:T(8,128)(2,1)} %emitted.1, s32[1,2,64]{2,1,0:T(2,128)} %levels.1, s32[1,6,2,64]{3,2,1,0:T(2,128)} %bitcast.4, f32[1,6,2,64]{3,2,1,0:T(2,128)} %bitcast.5, bf16[1,1,2048,768]{3,2,1,0:T(8,128)(2,1)} %w_gate.1, bf16[1,1,2048,768]{3,2,1,0:T(8,128)(2,1)} %w_up.1, ...), custom_call_target="tpu_custom_call" | custom-call | tf_op jit(solution)/shard_map/pallas_call | solution.py:410
  83.8 0.8 copy.10
